TPU v7x, 32 devices: a whole 2x2x4 slice. The times are simulated.
32 devices in a mesh: tm: 2 (over x), grid: 16 (over z, y, core).
Axes of the slice: x: 2, y: 2, z: 4, core: 2. Of those that a mesh axis runs over, the one named last changes fastest.
Arguments:
- occupied_green: bfloat16 [2, 1024, 1024], P('tm', 'grid'), may hold values from -0.005859375 to 0.005859375
- empty_green: bfloat16 [2, 1024, 1024], P('tm', 'grid'), may hold values from -0.005859375 to 0.005859375
- basis: bfloat16 [12288, 1024], P('grid'), may hold values from -8 to 8
- time_weights: float32 [2, 2], replicated, may hold values from 0.25 to 1
Outputs:
- polarizability: float32 [2, 1024, 1024], P('tm', 'grid')
All inputs are finite; a program needn't handle non-finite values.
Results may differ from a plain program's by a relative error of at most 0.0012.
Values may be sent and summed in bfloat16 or wider, within the bound.
A program may use at most 128 MiB of HBM per device.

v0:
```python
import jax
import jax.numpy as jnp
from jax import lax
from jax.sharding import PartitionSpec as P

NR = 12288
NB = 1024


def weigh_times(time_weights, block_list, scale_factor):
    time_count = len(block_list)
    group_index = lax.axis_index("tm")
    weights_local = lax.dynamic_slice_in_dim(time_weights, group_index * time_count, time_count, 1)
    accum = weights_local[:, 0, None, None] * block_list[0][None]
    return scale_factor * accum


def step_size(piece_rows):
    return max((divisor for divisor in range(1, 2049) if piece_rows % divisor == 0))


def shards(occupied_green, empty_green, basis, time_weights):
    stacked = jnp.stack([occupied_green, empty_green])
    time_count = occupied_green.shape[0]
    coef_block = occupied_green.shape[1]
    row_total = basis.shape[0]
    scale_factor = 1.0 / NR

    def make_accumulate(combined_rows):

        def accumulate(running, basis_piece, first_row):
            piece_rows = basis_piece.shape[0]
            step_rows = step_size(piece_rows)

            def one_step(step_index, inner):
                basis_subpart = lax.dynamic_slice_in_dim(
                    basis_piece, step_index * step_rows, step_rows, 0
                )
                real_pair = jnp.einsum(
                    "qoa,ba->qob", combined_rows, basis_subpart, preferred_element_type=jnp.float32
                )
                product = (real_pair[0] * real_pair[1]).astype(jnp.bfloat16)
                return inner + jnp.dot(product, basis_subpart, preferred_element_type=jnp.float32)

            return lax.fori_loop(0, piece_rows // step_rows, one_step, running)

        return accumulate

    initial = jnp.zeros((time_count * row_total, NB), jnp.float32)
    projected = jnp.einsum(
        "sl,ftkl->ftsk",
        basis,
        lax.all_gather(stacked, "grid", axis=2, tiled=True),
        preferred_element_type=jnp.float32,
    ).astype(jnp.bfloat16)
    combined_rows = projected.reshape(2, time_count * row_total, NB)
    accumulate = make_accumulate(combined_rows)
    summed = accumulate(initial, lax.all_gather(basis, "grid", axis=0, tiled=True), jnp.int32(0))
    back_half = summed.astype(jnp.bfloat16).reshape(time_count, row_total, NB)
    coef_rows = lax.psum_scatter(
        jnp.einsum("tsk,sl->ktl", back_half, basis, preferred_element_type=jnp.float32).reshape(
            lax.axis_size("grid") * coef_block, time_count * NB
        ),
        "grid",
        scatter_dimension=0,
        tiled=True,
    ).reshape(coef_block, time_count, NB)
    block_list = [coef_rows[:, 0]]
    result = lax.psum_scatter(
        weigh_times(time_weights, block_list, scale_factor), "tm", scatter_dimension=0, tiled=True
    )
    return result


def solution(mesh):
    in_specs = (P("tm", "grid", None), P("tm", "grid", None), P("grid", None), P())
    out_specs = P("tm", "grid", None)
    return jax.shard_map(shards, mesh=mesh, in_specs=in_specs, out_specs=out_specs, check_vma=False)
```

profile of v0, /device:TPU:0, one launch (start us, length us, event | category | flops | bytes accessed | tf_op | source)
XLA Modules:
  0.0 431.6 jit_solution(16188916720244867342)
XLA Ops:
  6.5 0.0 copy-start
  6.5 0.0 all-gather.5.cloned.1.call-start
  6.5 1.7 pad_maximum_fusion
  8.2 0.0 all-gather.5.cloned.1.call-update
  8.3 0.0 all-gather.3.cloned.1.call-start
  8.3 0.7 all-gather.3.cloned.1.call-update
  9.0 0.0 reduce-scatter.3.cloned.1.call-start
  9.1 53.6 %all-gather.5.cloned.1.call-done = bf16[2,1,1024,1024]{3,2,0,1:T(8,128)(2,1)} async-done(((bf16[2,1,64,1024]{3,2,0,1:T(8,128)(2,1)}), bf16[2,1,1024,1024]{3,2,0,1:T(8,128)(2,1)}) %all-gather.5.cloned.1.call-update) | async-done | bytes 4194320 | tf_op jit(solution)/shard_map/all_gather | solution.py:53
  62.7 7.9 %convert_bitcast_fusion = bf16[2,768,1024]{1,2,0:T(8,128)(2,1)} fusion(bf16[2,1,1024,1024]{3,2,0,1:T(8,128)(2,1)} %all-gather.5.cloned.1.call-done, bf16[768,1024]{1,0:T(8,128)(2,1)} %param.8), kind=kOutput, calls=%fused_computation.13 | convolution fusion | flops 3222798336 | bytes 8912896 | tf_op jit(solution)/shard_map/sl,ftkl->ftsk/dot_general | solution.py:50
  70.5 3.2 copy.5
  73.8 117.6 %all-gather.3.cloned.1.call-done = bf16[12288,1024]{1,0:T(8,128)(2,1)} async-done(((bf16[768,1024]{1,0:T(8,128)(2,1)}), bf16[12288,1024]{1,0:T(8,128)(2,1)}) %all-gather.3.cloned.1.call-update) | async-done | bytes 25165840 | tf_op jit(solution)/shard_map/all_gather | solution.py:58
  191.3 138.8 %while.14 = (s32[]{:T(128)}, f32[768,1024]{1,0:T(8,128)}, bf16[12288,1024]{1,0:T(8,128)(2,1)}, bf16[2,768,1024]{2,1,0:T(8,128)(2,1)S(1)}, s32[]{:T(128)}, /*index=5*/s32[]{:T(128)}, s32[]{:T(128)}, s32[]{:T(128)}) while((s32[]{:T(128)}, f32[768,1024]{1,0:T(8,128)}, bf16[12288,1024]{1,0:T(8,128)(2,1)}, ...), condition=%wide.region_1.0_spmd.clone, body=%wide.region_0.0_spmd.clone.sunk | while | flops 9668395008 | bytes 42991772 | solution.py:45
  191.4 11.5 %convolution_bitcast_fusion.2 = f32[2,768,2048]{1,2,0:T(8,128)} fusion(bf16[2,768,1024]{2,1,0:T(8,128)(2,1)S(1)} %get-tuple-element.156, bf16[12288,1024]{1,0:T(8,128)(2,1)} %get-tuple-element.155, s32[]{:T(128)S(6)} %select_n.13), kind=kOutput, calls=%fused_computation.2.clone.1 | convolution fusion | flops 6442450944 | bytes 19922948 | tf_op jit(solution)/shard_map/while/body/eval_jaxpr/qoa,ba->qob/dot_general | solution.py:39
  202.9 10.9 %select_add_fusion.2 = f32[768,1024]{1,0:T(8,128)} fusion(f32[768,1024]{1,0:T(8,128)} %get-tuple-element.146, bf16[12288,1024]{1,0:T(8,128)(2,1)} %get-tuple-element.155, s32[]{:T(128)S(6)} %select_n.13, f32[2,768,2048]{1,2,0:T(8,128)} %convolution_bitcast_fusion.2, pred[]{:T(512)S(6)} %compare.3), kind=kOutput, calls=%fused_computation.8.clone.1 | convolution fusion | flops 3225944064 | bytes 23068676 | tf_op jit(solution)/shard_map/while/body/eval_jaxpr/dot_general | solution.py:43
  213.7 11.5 %convolution_bitcast_fusion.2 = f32[2,768,2048]{1,2,0:T(8,128)} fusion(bf16[2,768,1024]{2,1,0:T(8,128)(2,1)S(1)} %get-tuple-element.156, bf16[12288,1024]{1,0:T(8,128)(2,1)} %get-tuple-element.155, s32[]{:T(128)S(6)} %select_n.13), kind=kOutput, calls=%fused_computation.2.clone.1 | convolution fusion | flops 6442450944 | bytes 19922948 | tf_op jit(solution)/shard_map/while/body/eval_jaxpr/qoa,ba->qob/dot_general | solution.py:39
  225.2 11.8 %select_add_fusion.2 = f32[768,1024]{1,0:T(8,128)} fusion(f32[768,1024]{1,0:T(8,128)} %get-tuple-element.146, bf16[12288,1024]{1,0:T(8,128)(2,1)} %get-tuple-element.155, s32[]{:T(128)S(6)} %select_n.13, f32[2,768,2048]{1,2,0:T(8,128)} %convolution_bitcast_fusion.2, pred[]{:T(512)S(6)} %compare.3), kind=kOutput, calls=%fused_computation.8.clone.1 | convolution fusion | flops 3225944064 | bytes 23068676 | tf_op jit(solution)/shard_map/while/body/eval_jaxpr/dot_general | solution.py:43
  237.0 11.5 %convolution_bitcast_fusion.2 = f32[2,768,2048]{1,2,0:T(8,128)} fusion(bf16[2,768,1024]{2,1,0:T(8,128)(2,1)S(1)} %get-tuple-element.156, bf16[12288,1024]{1,0:T(8,128)(2,1)} %get-tuple-element.155, s32[]{:T(128)S(6)} %select_n.13), kind=kOutput, calls=%fused_computation.2.clone.1 | convolution fusion | flops 6442450944 | bytes 19922948 | tf_op jit(solution)/shard_map/while/body/eval_jaxpr/qoa,ba->qob/dot_general | solution.py:39
  248.5 11.8 %select_add_fusion.2 = f32[768,1024]{1,0:T(8,128)} fusion(f32[768,1024]{1,0:T(8,128)} %get-tuple-element.146, bf16[12288,1024]{1,0:T(8,128)(2,1)} %get-tuple-element.155, s32[]{:T(128)S(6)} %select_n.13, f32[2,768,2048]{1,2,0:T(8,128)} %convolution_bitcast_fusion.2, pred[]{:T(512)S(6)} %compare.3), kind=kOutput, calls=%fused_computation.8.clone.1 | convolution fusion | flops 3225944064 | bytes 23068676 | tf_op jit(solution)/shard_map/while/body/eval_jaxpr/dot_general | solution.py:43
  260.3 11.5 %convolution_bitcast_fusion.2 = f32[2,768,2048]{1,2,0:T(8,128)} fusion(bf16[2,768,1024]{2,1,0:T(8,128)(2,1)S(1)} %get-tuple-element.156, bf16[12288,1024]{1,0:T(8,128)(2,1)} %get-tuple-element.155, s32[]{:T(128)S(6)} %select_n.13), kind=kOutput, calls=%fused_computation.2.clone.1 | convolution fusion | flops 6442450944 | bytes 19922948 | tf_op jit(solution)/shard_map/while/body/eval_jaxpr/qoa,ba->qob/dot_general | solution.py:39
  271.8 11.8 %select_add_fusion.2 = f32[768,1024]{1,0:T(8,128)} fusion(f32[768,1024]{1,0:T(8,128)} %get-tuple-element.146, bf16[12288,1024]{1,0:T(8,128)(2,1)} %get-tuple-element.155, s32[]{:T(128)S(6)} %select_n.13, f32[2,768,2048]{1,2,0:T(8,128)} %convolution_bitcast_fusion.2, pred[]{:T(512)S(6)} %compare.3), kind=kOutput, calls=%fused_computation.8.clone.1 | convolution fusion | flops 3225944064 | bytes 23068676 | tf_op jit(solution)/shard_map/while/body/eval_jaxpr/dot_general | solution.py:43
  283.6 11.5 %convolution_bitcast_fusion.2 = f32[2,768,2048]{1,2,0:T(8,128)} fusion(bf16[2,768,1024]{2,1,0:T(8,128)(2,1)S(1)} %get-tuple-element.156, bf16[12288,1024]{1,0:T(8,128)(2,1)} %get-tuple-element.155, s32[]{:T(128)S(6)} %select_n.13), kind=kOutput, calls=%fused_computation.2.clone.1 | convolution fusion | flops 6442450944 | bytes 19922948 | tf_op jit(solution)/shard_map/while/body/eval_jaxpr/qoa,ba->qob/dot_general | solution.py:39
  295.1 11.8 %select_add_fusion.2 = f32[768,1024]{1,0:T(8,128)} fusion(f32[768,1024]{1,0:T(8,128)} %get-tuple-element.146, bf16[12288,1024]{1,0:T(8,128)(2,1)} %get-tuple-element.155, s32[]{:T(128)S(6)} %select_n.13, f32[2,768,2048]{1,2,0:T(8,128)} %convolution_bitcast_fusion.2, pred[]{:T(512)S(6)} %compare.3), kind=kOutput, calls=%fused_computation.8.clone.1 | convolution fusion | flops 3225944064 | bytes 23068676 | tf_op jit(solution)/shard_map/while/body/eval_jaxpr/dot_general | solution.py:43
  306.9 11.5 %convolution_bitcast_fusion.2 = f32[2,768,2048]{1,2,0:T(8,128)} fusion(bf16[2,768,1024]{2,1,0:T(8,128)(2,1)S(1)} %get-tuple-element.156, bf16[12288,1024]{1,0:T(8,128)(2,1)} %get-tuple-element.155, s32[]{:T(128)S(6)} %select_n.13), kind=kOutput, calls=%fused_computation.2.clone.1 | convolution fusion | flops 6442450944 | bytes 19922948 | tf_op jit(solution)/shard_map/while/body/eval_jaxpr/qoa,ba->qob/dot_general | solution.py:39
  318.4 11.8 %select_add_fusion.2 = f32[768,1024]{1,0:T(8,128)} fusion(f32[768,1024]{1,0:T(8,128)} %get-tuple-element.146, bf16[12288,1024]{1,0:T(8,128)(2,1)} %get-tuple-element.155, s32[]{:T(128)S(6)} %select_n.13, f32[2,768,2048]{1,2,0:T(8,128)} %convolution_bitcast_fusion.2, pred[]{:T(512)S(6)} %compare.3), kind=kOutput, calls=%fused_computation.8.clone.1 | convolution fusion | flops 3225944064 | bytes 23068676 | tf_op jit(solution)/shard_map/while/body/eval_jaxpr/dot_general | solution.py:43
  330.2 6.1 %fusion.18 = f32[1024,1024]{1,0:T(8,128)} fusion(bf16[768,1024]{1,0:T(8,128)(2,1)} %param.8, f32[768,1024]{1,0:T(8,128)} %get-tuple-element.84), kind=kOutput, calls=%fused_computation.15 | convolution fusion | flops 1611399168 | bytes 8912896 | tf_op jit(solution)/shard_map/tsk,sl->ktl/dot_general | solution.py:61
  336.3 0.0 reduce-scatter.3.cloned.1.call-update
  336.3 0.0 reduce-scatter.5.cloned.1.call-start
  336.4 0.0 copy-done
  336.4 0.2 dynamic-slice_reduce_fusion
  336.6 72.7 %reduce-scatter.3.cloned.1.call-done = f32[64,1024]{1,0:T(8,128)} async-done(((f32[1024,1024]{1,0:T(8,128)}), f32[64,1024]{1,0:T(8,128)}) %reduce-scatter.3.cloned.1.call-update) | async-done | bytes 262160 | tf_op jit(solution)/shard_map/reduce_scatter | solution.py:60
  409.2 1.9 multiply_multiply_fusion
  411.1 0.0 reduce-scatter.5.cloned.1.call-update
  411.1 13.9 %reduce-scatter.5.cloned.1.call-done = f32[1,64,1024]{2,1,0:T(8,128)} async-done(((f32[2,64,1024]{2,1,0:T(8,128)}), f32[1,64,1024]{2,1,0:T(8,128)}) %reduce-scatter.5.cloned.1.call-update) | async-done | bytes 262160 | tf_op jit(solution)/shard_map/reduce_scatter | solution.py:69
  (1 shorter events, 0.0 us)
Async XLA Ops:
  6.5 329.8 %copy-start = (f32[2,2]{1,0:T(2,128)S(1)}, f32[2,2]{1,0:T(2,128)}, u32[]{:S(2)}) copy-start(f32[2,2]{1,0:T(2,128)} %param.9) | copy-start | bytes 52
  6.5 56.1 %all-gather.5.cloned.1.call-start = ((), (), s32[]{:S(2)}) async-start(), calls=%async_computation.3 | async-start | bytes 4456448 | tf_op jit(solution)/shard_map/all_gather | solution.py:53
  8.3 183.1 %all-gather.3.cloned.1.call-start = ((), (), s32[]{:S(2)}) async-start(), calls=%async_computation.2 | async-start | bytes 26738688 | tf_op jit(solution)/shard_map/all_gather | solution.py:58
  9.0 400.2 %reduce-scatter.3.cloned.1.call-start = ((), (), s32[]{:S(2)}) async-start(), calls=%async_computation.4 | async-start | bytes 4456448 | tf_op jit(solution)/shard_map/reduce_scatter | solution.py:60
  336.3 88.8 %reduce-scatter.5.cloned.1.call-start = ((), (), s32[]{:S(2)}) async-start(), calls=%async_computation.5 | async-start | bytes 786432 | tf_op jit(solution)/shard_map/reduce_scatter | solution.py:69
Sparse Core Ops, SparseCore 0:
  9.5 53.1 all-gather.4
  64.3 127.0 all-gather.2
  336.4 72.7 reduce-scatter.2
  411.3 13.6 reduce-scatter.4
where the time goes:
time: 432 us
  waiting for transfers between devices  259 us (60%)
  matrix products  153 us (35%)
  between operations  13.2 us (3%)
    all_gather x1, waiting for transfers between devices, shards(): lax.all_gather(basis, 'grid', axis=0, tiled=True)  118 us
    reduce_scatter x1, waiting for transfers between devices, shards(): lax.psum_scatter(jnp.einsum('tsk,sl->ktl', back_half, basis, preferred_el...  72.7 us
    dot_general x6, matrix products, one_step(): jnp.dot(product, basis_subpart, preferred_element_type=jnp.float32)  69.8 us
    dot_general x6, matrix products, one_step(): jnp.einsum('qoa,ba->qob', combined_rows, basis_subpart, preferred_element...  69 us
    all_gather x1, waiting for transfers between devices, shards(): lax.all_gather(stacked, 'grid', axis=2, tiled=True)  53.6 us
    reduce_scatter x1, waiting for transfers between devices, shards(): lax.psum_scatter(weigh_times(time_weights, block_list, scale_factor), 'tm...  13.9 us
  transfers between devices with their start and end apart: 4, of which 4 were waited for; matrix products, arithmetic and copies ran while one was open for 3% of the time, Pallas kernels for 0%

commit v1 on v0

--- a/solution.py
+++ b/solution.py
@@ -5,6 +5,24 @@
 
 NR = 12288
 NB = 1024
+
+
+def work_around(value, axis, dim, apply, out_dim):
+    peers, index, rows = (lax.axis_size(axis), lax.axis_index(axis), value.shape[dim])
+    right = [(i, (i + 1) % peers) for i in range(peers)]
+    held, out = (value, None)
+    for step in range(peers):
+        owner = (index - step) % peers
+        coming = lax.ppermute(held, axis, right) if step < peers - 1 else None
+        made = apply(held, owner * rows)
+        length = made.shape[out_dim]
+        if out is None:
+            out = jnp.zeros(
+                (*made.shape[:out_dim], peers * length, *made.shape[out_dim + 1 :]), made.dtype
+            )
+        out = lax.dynamic_update_slice_in_dim(out, made, owner * length, axis=out_dim)
+        held = coming
+    return out
 
 
 def weigh_times(time_weights, block_list, scale_factor):
@@ -47,11 +65,14 @@
         return accumulate
 
     initial = jnp.zeros((time_count * row_total, NB), jnp.float32)
-    projected = jnp.einsum(
-        "sl,ftkl->ftsk",
-        basis,
-        lax.all_gather(stacked, "grid", axis=2, tiled=True),
-        preferred_element_type=jnp.float32,
+    projected = work_around(
+        stacked,
+        "grid",
+        2,
+        lambda own_block, start: jnp.einsum(
+            "sl,ftkl->ftsk", basis, own_block, preferred_element_type=jnp.float32
+        ),
+        3,
     ).astype(jnp.bfloat16)
     combined_rows = projected.reshape(2, time_count * row_total, NB)
     accumulate = make_accumulate(combined_rows)

time: 432 us -> 435 us (level)
  local copies, waits for them, and re-layouts: 3.4 us -> 111 us
  waiting for transfers between devices: 259 us -> 190 us
  matrix products: 153 us -> 112 us
    all_gather x1, waiting for transfers between devices: 118 us -> 0.01 us  [shards(): lax.all_gather(basis, 'grid', axis=0, tiled=True)]
    ppermute x0 -> x15, waiting for transfers between devices: none -> 100 us  [work_around(): coming = lax.ppermute(held, axis, right) if step < peers - 1 else None]
    dynamic_update_slice x0 -> x16, local copies, waits for them, and re-layouts: none -> 93.8 us  [work_around(): lax.dynamic_update_slice_in_dim(out, made, owner * length, axis=out_dim)]
    all_gather x1 -> x0, waiting for transfers between devices: 53.6 us -> none  [shards(): lax.all_gather(stacked, 'grid', axis=2, tiled=True)]
    dot_general x6, matrix products: 69.8 us -> 33.9 us  [one_step(): jnp.dot(product, basis_subpart, preferred_element_type=jnp.float32)]
    dot_general x6, matrix products: 69 us -> 57.6 us  [one_step(): jnp.einsum('qoa,ba->qob', combined_rows, basis_subpart, preferred_element...]
    while x0 -> x24, local copies, waits for them, and re-layouts: none -> 10.1 us
    dot_general x1 -> x16, matrix products: 7.87 us -> 15.2 us  [shards(): jnp.einsum('sl,ftkl->ftsk', basis, own_block, preferred_element_type=jnp....]
  transfers between devices with their start and end apart: 4 -> 18, of which waited for: 4 -> 12; matrix products, arithmetic and copies ran while one was open for 3% -> 27% of each run, Pallas kernels for 0% -> 0%
where the time goes in v1:
time: 435 us; the launch traced here: 431 us
  waiting for transfers between devices  190 us (44%)
  matrix products  112 us (26%)
  local copies, waits for them, and re-layouts  111 us (26%)
  between operations  13.5 us (3%)
    ppermute x15, waiting for transfers between devices, work_around(): coming = lax.ppermute(held, axis, right) if step < peers - 1 else None  100 us
    dynamic_update_slice x16, local copies, waits for them, and re-layouts, work_around(): lax.dynamic_update_slice_in_dim(out, made, owner * length, axis=out_dim)  93.8 us
    reduce_scatter x1, waiting for transfers between devices, shards(): lax.psum_scatter(jnp.einsum('tsk,sl->ktl', back_half, basis, preferred_el...  75.7 us
    dot_general x6, matrix products, one_step(): jnp.einsum('qoa,ba->qob', combined_rows, basis_subpart, preferred_element...  57.6 us
    dot_general x6, matrix products, one_step(): jnp.dot(product, basis_subpart, preferred_element_type=jnp.float32)  33.9 us
    dot_general x16, matrix products, shards(): jnp.einsum('sl,ftkl->ftsk', basis, own_block, preferred_element_type=jnp....  15.2 us
    reduce_scatter x1, waiting for transfers between devices, shards(): lax.psum_scatter(weigh_times(time_weights, block_list, scale_factor), 'tm...  14.1 us
    while x24, local copies, waits for them, and re-layouts  10.1 us
  transfers between devices with their start and end apart: 18, of which 12 were waited for; matrix products, arithmetic and copies ran while one was open for 27% of the time, Pallas kernels for 0%

profile of v1, /device:TPU:0, one launch (start us, length us, event | category | flops | bytes accessed | tf_op | source)
XLA Modules:
  0.0 431.3 jit_solution(16850558769675127698)
XLA Ops:
  8.9 9.0 %collective-permute-done = bf16[2,1,64,1024]{3,2,0,1:T(8,128)(2,1)S(1)} collective-permute-done((bf16[2,1,64,1024]{3,2,0,1:T(8,128)(2,1)S(1)}, bf16[2,1,64,1024]{3,2,0,1:T(8,128)(2,1)S(1)}, u32[]{:S(2)}, u32[]{:S(2)}) %collective-permute-start) | collective-permute-done | bytes 262176 | tf_op jit(solution)/shard_map/ppermute | solution.py:16
  18.6 13.2 %collective-permute-done.1 = bf16[2,1,64,1024]{3,2,0,1:T(8,128)(2,1)S(1)} collective-permute-done((bf16[2,1,64,1024]{3,2,0,1:T(8,128)(2,1)S(1)}, bf16[2,1,64,1024]{3,2,0,1:T(8,128)(2,1)S(1)}, u32[]{:S(2)}, u32[]{:S(2)}) %collective-permute-start.1) | collective-permute-done | bytes 262176 | tf_op jit(solution)/shard_map/ppermute | solution.py:16
  32.5 13.5 %collective-permute-done.2 = bf16[2,1,64,1024]{3,2,0,1:T(8,128)(2,1)S(1)} collective-permute-done((bf16[2,1,64,1024]{3,2,0,1:T(8,128)(2,1)S(1)}, bf16[2,1,64,1024]{3,2,0,1:T(8,128)(2,1)S(1)}, u32[]{:S(2)}, u32[]{:S(2)}) %collective-permute-start.2) | collective-permute-done | bytes 262176 | tf_op jit(solution)/shard_map/ppermute | solution.py:16
  46.0 14.2 %collective-permute-done.3 = bf16[2,1,64,1024]{3,2,0,1:T(8,128)(2,1)S(1)} collective-permute-done((bf16[2,1,64,1024]{3,2,0,1:T(8,128)(2,1)S(1)}, bf16[2,1,64,1024]{3,2,0,1:T(8,128)(2,1)S(1)}, u32[]{:S(2)}, u32[]{:S(2)}) %collective-permute-start.3) | collective-permute-done | bytes 262176 | tf_op jit(solution)/shard_map/ppermute | solution.py:16
  60.3 14.2 %collective-permute-done.4 = bf16[2,1,64,1024]{3,2,0,1:T(8,128)(2,1)S(1)} collective-permute-done((bf16[2,1,64,1024]{3,2,0,1:T(8,128)(2,1)S(1)}, bf16[2,1,64,1024]{3,2,0,1:T(8,128)(2,1)S(1)}, u32[]{:S(2)}, u32[]{:S(2)}) %collective-permute-start.4) | collective-permute-done | bytes 262176 | tf_op jit(solution)/shard_map/ppermute | solution.py:16
  74.5 14.2 %collective-permute-done.5 = bf16[2,1,64,1024]{3,2,0,1:T(8,128)(2,1)S(1)} collective-permute-done((bf16[2,1,64,1024]{3,2,0,1:T(8,128)(2,1)S(1)}, bf16[2,1,64,1024]{3,2,0,1:T(8,128)(2,1)S(1)}, u32[]{:S(2)}, u32[]{:S(2)}) %collective-permute-start.5) | collective-permute-done | bytes 262176 | tf_op jit(solution)/shard_map/ppermute | solution.py:16
  88.7 14.2 %collective-permute-done.6 = bf16[2,1,64,1024]{3,2,0,1:T(8,128)(2,1)S(1)} collective-permute-done((bf16[2,1,64,1024]{3,2,0,1:T(8,128)(2,1)S(1)}, bf16[2,1,64,1024]{3,2,0,1:T(8,128)(2,1)S(1)}, u32[]{:S(2)}, u32[]{:S(2)}) %collective-permute-start.6) | collective-permute-done | bytes 262176 | tf_op jit(solution)/shard_map/ppermute | solution.py:16
  104.0 2.1 broadcast_in_dim.7
  106.1 5.5 %dynamic_update_slice.48 = bf16[2,1,768,1024]{3,2,0,1:T(8,128)(2,1)} dynamic-update-slice(bf16[2,1,768,1024]{3,2,0,1:T(8,128)(2,1)} %broadcast_in_dim.7, bf16[2,1,768,64]{3,2,0,1:T(8,128)(2,1)S(1)} %copy.5, s32[]{:T(128)} %constant.140.clone.1, s32[]{:T(128)} %constant.140.clone.1, s32[]{:T(128)} %constant.140.clone.1, s32[]{:T(128)S(6)} %select_n.127) | dynamic-update-slice | bytes 393220 | tf_op jit(solution)/shard_map/dynamic_update_slice | solution.py:23
  111.6 5.6 %collective-permute-done.7 = bf16[2,1,64,1024]{3,2,0,1:T(8,128)(2,1)S(1)} collective-permute-done((bf16[2,1,64,1024]{3,2,0,1:T(8,128)(2,1)S(1)}, bf16[2,1,64,1024]{3,2,0,1:T(8,128)(2,1)S(1)}, u32[]{:S(2)}, u32[]{:S(2)}) %collective-permute-start.7) | collective-permute-done | bytes 262176 | tf_op jit(solution)/shard_map/ppermute | solution.py:16
  118.1 5.8 %dynamic_update_slice.49 = bf16[2,1,768,1024]{3,2,0,1:T(8,128)(2,1)} dynamic-update-slice(bf16[2,1,768,1024]{3,2,0,1:T(8,128)(2,1)} %dynamic_update_slice.48, bf16[2,1,768,64]{3,2,0,1:T(8,128)(2,1)S(1)} %copy.6, s32[]{:T(128)} %constant.140.clone.1, s32[]{:T(128)} %constant.140.clone.1, s32[]{:T(128)} %constant.140.clone.1, s32[]{:T(128)S(6)} %select_n.129) | dynamic-update-slice | bytes 393220 | tf_op jit(solution)/shard_map/dynamic_update_slice | solution.py:23
  125.7 4.9 %dynamic_update_slice.50 = bf16[2,1,768,1024]{3,2,0,1:T(8,128)(2,1)} dynamic-update-slice(bf16[2,1,768,1024]{3,2,0,1:T(8,128)(2,1)} %dynamic_update_slice.49, bf16[2,1,768,64]{3,2,0,1:T(8,128)(2,1)S(1)} %copy.7, s32[]{:T(128)} %constant.140.clone.1, s32[]{:T(128)} %constant.140.clone.1, s32[]{:T(128)} %constant.140.clone.1, s32[]{:T(128)S(6)} %select_n.131) | dynamic-update-slice | bytes 393220 | tf_op jit(solution)/shard_map/dynamic_update_slice | solution.py:23
  133.4 6.4 %dynamic_update_slice.51 = bf16[2,1,768,1024]{3,2,0,1:T(8,128)(2,1)} dynamic-update-slice(bf16[2,1,768,1024]{3,2,0,1:T(8,128)(2,1)} %dynamic_update_slice.50, bf16[2,1,768,64]{3,2,0,1:T(8,128)(2,1)S(1)} %copy.8, s32[]{:T(128)} %constant.140.clone.1, s32[]{:T(128)} %constant.140.clone.1, s32[]{:T(128)} %constant.140.clone.1, s32[]{:T(128)S(6)} %select_n.133) | dynamic-update-slice | bytes 393220 | tf_op jit(solution)/shard_map/dynamic_update_slice | solution.py:23
  140.7 5.5 %dynamic_update_slice.52 = bf16[2,1,768,1024]{3,2,0,1:T(8,128)(2,1)} dynamic-update-slice(bf16[2,1,768,1024]{3,2,0,1:T(8,128)(2,1)} %dynamic_update_slice.51, bf16[2,1,768,64]{3,2,0,1:T(8,128)(2,1)S(1)} %copy.9, s32[]{:T(128)} %constant.140.clone.1, s32[]{:T(128)} %constant.140.clone.1, s32[]{:T(128)} %constant.140.clone.1, s32[]{:T(128)S(6)} %select_n.135) | dynamic-update-slice | bytes 393220 | tf_op jit(solution)/shard_map/dynamic_update_slice | solution.py:23
  147.1 6.4 %dynamic_update_slice.53 = bf16[2,1,768,1024]{3,2,0,1:T(8,128)(2,1)} dynamic-update-slice(bf16[2,1,768,1024]{3,2,0,1:T(8,128)(2,1)} %dynamic_update_slice.52, bf16[2,1,768,64]{3,2,0,1:T(8,128)(2,1)S(1)} %copy.10, s32[]{:T(128)} %constant.140.clone.1, s32[]{:T(128)} %constant.140.clone.1, s32[]{:T(128)} %constant.140.clone.1, s32[]{:T(128)S(6)} %select_n.137) | dynamic-update-slice | bytes 393220 | tf_op jit(solution)/shard_map/dynamic_update_slice | solution.py:23
  154.4 5.5 %dynamic_update_slice.54 = bf16[2,1,768,1024]{3,2,0,1:T(8,128)(2,1)} dynamic-update-slice(bf16[2,1,768,1024]{3,2,0,1:T(8,128)(2,1)} %dynamic_update_slice.53, bf16[2,1,768,64]{3,2,0,1:T(8,128)(2,1)S(1)} %copy.11, s32[]{:T(128)} %constant.140.clone.1, s32[]{:T(128)} %constant.140.clone.1, s32[]{:T(128)} %constant.140.clone.1, s32[]{:T(128)S(6)} %select_n.139) | dynamic-update-slice | bytes 393220 | tf_op jit(solution)/shard_map/dynamic_update_slice | solution.py:23
  161.6 6.4 %dynamic_update_slice.55 = bf16[2,1,768,1024]{3,2,0,1:T(8,128)(2,1)} dynamic-update-slice(bf16[2,1,768,1024]{3,2,0,1:T(8,128)(2,1)} %dynamic_update_slice.54, bf16[2,1,768,64]{3,2,0,1:T(8,128)(2,1)S(1)} %copy.12, s32[]{:T(128)} %constant.140.clone.1, s32[]{:T(128)} %constant.140.clone.1, s32[]{:T(128)} %constant.140.clone.1, s32[]{:T(128)S(6)} %select_n.141) | dynamic-update-slice | bytes 393220 | tf_op jit(solution)/shard_map/dynamic_update_slice | solution.py:23
  168.8 5.5 %dynamic_update_slice.56 = bf16[2,1,768,1024]{3,2,0,1:T(8,128)(2,1)} dynamic-update-slice(bf16[2,1,768,1024]{3,2,0,1:T(8,128)(2,1)} %dynamic_update_slice.55, bf16[2,1,768,64]{3,2,0,1:T(8,128)(2,1)S(1)} %copy.13, s32[]{:T(128)} %constant.140.clone.1, s32[]{:T(128)} %constant.140.clone.1, s32[]{:T(128)} %constant.140.clone.1, s32[]{:T(128)S(6)} %select_n.143) | dynamic-update-slice | bytes 393220 | tf_op jit(solution)/shard_map/dynamic_update_slice | solution.py:23
  176.2 6.3 %dynamic_update_slice.57 = bf16[2,1,768,1024]{3,2,0,1:T(8,128)(2,1)} dynamic-update-slice(bf16[2,1,768,1024]{3,2,0,1:T(8,128)(2,1)} %dynamic_update_slice.56, bf16[2,1,768,64]{3,2,0,1:T(8,128)(2,1)S(1)} %copy.14, s32[]{:T(128)} %constant.140.clone.1, s32[]{:T(128)} %constant.140.clone.1, s32[]{:T(128)} %constant.140.clone.1, s32[]{:T(128)S(6)} %select_n.145) | dynamic-update-slice | bytes 393220 | tf_op jit(solution)/shard_map/dynamic_update_slice | solution.py:23
  184.3 5.5 %dynamic_update_slice.58 = bf16[2,1,768,1024]{3,2,0,1:T(8,128)(2,1)} dynamic-update-slice(bf16[2,1,768,1024]{3,2,0,1:T(8,128)(2,1)} %dynamic_update_slice.57, bf16[2,1,768,64]{3,2,0,1:T(8,128)(2,1)S(1)} %copy.15, s32[]{:T(128)} %constant.140.clone.1, s32[]{:T(128)} %constant.140.clone.1, s32[]{:T(128)} %constant.140.clone.1, s32[]{:T(128)S(6)} %select_n.147) | dynamic-update-slice | bytes 393220 | tf_op jit(solution)/shard_map/dynamic_update_slice | solution.py:23
  190.7 6.3 %dynamic_update_slice.59 = bf16[2,1,768,1024]{3,2,0,1:T(8,128)(2,1)} dynamic-update-slice(bf16[2,1,768,1024]{3,2,0,1:T(8,128)(2,1)} %dynamic_update_slice.58, bf16[2,1,768,64]{3,2,0,1:T(8,128)(2,1)S(1)} %copy.16, s32[]{:T(128)} %constant.140.clone.1, s32[]{:T(128)} %constant.140.clone.1, s32[]{:T(128)} %constant.140.clone.1, s32[]{:T(128)S(6)} %select_n.149) | dynamic-update-slice | bytes 393220 | tf_op jit(solution)/shard_map/dynamic_update_slice | solution.py:23
  198.0 5.5 %dynamic_update_slice.60 = bf16[2,1,768,1024]{3,2,0,1:T(8,128)(2,1)} dynamic-update-slice(bf16[2,1,768,1024]{3,2,0,1:T(8,128)(2,1)} %dynamic_update_slice.59, bf16[2,1,768,64]{3,2,0,1:T(8,128)(2,1)S(1)} %copy.17, s32[]{:T(128)} %constant.140.clone.1, s32[]{:T(128)} %constant.140.clone.1, s32[]{:T(128)} %constant.140.clone.1, s32[]{:T(128)S(6)} %select_n.151) | dynamic-update-slice | bytes 393220 | tf_op jit(solution)/shard_map/dynamic_update_slice | solution.py:23
  204.3 6.4 %dynamic_update_slice.61 = bf16[2,1,768,1024]{3,2,0,1:T(8,128)(2,1)} dynamic-update-slice(bf16[2,1,768,1024]{3,2,0,1:T(8,128)(2,1)} %dynamic_update_slice.60, bf16[2,1,768,64]{3,2,0,1:T(8,128)(2,1)S(1)} %copy.18, s32[]{:T(128)} %constant.140.clone.1, s32[]{:T(128)} %constant.140.clone.1, s32[]{:T(128)} %constant.140.clone.1, s32[]{:T(128)S(6)} %select_n.153) | dynamic-update-slice | bytes 393220 | tf_op jit(solution)/shard_map/dynamic_update_slice | solution.py:23
  212.5 5.5 %dynamic_update_slice.62 = bf16[2,1,768,1024]{3,2,0,1:T(8,128)(2,1)} dynamic-update-slice(bf16[2,1,768,1024]{3,2,0,1:T(8,128)(2,1)} %dynamic_update_slice.61, bf16[2,1,768,64]{3,2,0,1:T(8,128)(2,1)S(1)} %copy.19, s32[]{:T(128)} %constant.140.clone.1, s32[]{:T(128)} %constant.140.clone.1, s32[]{:T(128)} %constant.140.clone.1, s32[]{:T(128)S(6)} %select_n.155) | dynamic-update-slice | bytes 393220 | tf_op jit(solution)/shard_map/dynamic_update_slice | solution.py:23
  219.0 6.3 %dynamic_update_slice.63 = bf16[2,1,768,1024]{3,2,0,1:T(8,128)(2,1)} dynamic-update-slice(bf16[2,1,768,1024]{3,2,0,1:T(8,128)(2,1)} %dynamic_update_slice.62, bf16[2,1,768,64]{3,2,0,1:T(8,128)(2,1)S(1)} %copy.20, s32[]{:T(128)} %constant.140.clone.1, s32[]{:T(128)} %constant.140.clone.1, s32[]{:T(128)} %constant.140.clone.1, s32[]{:T(128)S(6)} %select_n.157) | dynamic-update-slice | bytes 393220 | tf_op jit(solution)/shard_map/dynamic_update_slice | solution.py:23
  225.3 101.8 %while.14 = (s32[]{:T(128)}, f32[768,1024]{1,0:T(8,128)}, bf16[12288,1024]{1,0:T(8,128)(2,1)}, bf16[2,768,1024]{2,1,0:T(8,128)(2,1)}, s32[]{:T(128)}, /*index=5*/s32[]{:T(128)}, s32[]{:T(128)}, s32[]{:T(128)}) while((s32[]{:T(128)}, f32[768,1024]{1,0:T(8,128)}, bf16[12288,1024]{1,0:T(8,128)(2,1)}, bf16[2,768,1024]{2,1,0:T(8,128)(2,1)}, ...), condition=%wide.region_1.2_spmd.clone, body=%wide.region_0.1_spmd.clone.sunk | while | flops 9668395008 | bytes 68157656 | solution.py:63
  225.3 9.6 %convolution_bitcast_fusion.2 = f32[2,768,2048]{1,2,0:T(8,128)S(1)} fusion(bf16[2,768,1024]{2,1,0:T(8,128)(2,1)} %get-tuple-element.152, bf16[12288,1024]{1,0:T(8,128)(2,1)} %get-tuple-element.151, s32[]{:T(128)S(6)} %select_n.160), kind=kOutput, calls=%fused_computation.2.clone.1 | convolution fusion | flops 6442450944 | bytes 19922948 | tf_op jit(solution)/shard_map/while/body/eval_jaxpr/qoa,ba->qob/dot_general | solution.py:57
  234.9 5.7 %select_add_fusion.2 = f32[768,1024]{1,0:T(8,128)S(1)} fusion(f32[768,1024]{1,0:T(8,128)S(1)} %copy-done.10, bf16[12288,1024]{1,0:T(8,128)(2,1)} %get-tuple-element.151, s32[]{:T(128)S(6)} %select_n.160, f32[2,768,2048]{1,2,0:T(8,128)S(1)} %convolution_bitcast_fusion.2, pred[]{:T(512)S(6)} %compare.19), kind=kOutput, calls=%fused_computation.8.clone.1 | convolution fusion | flops 3225944064 | bytes 23068676 | tf_op jit(solution)/shard_map/while/body/eval_jaxpr/dot_general | solution.py:61
  240.6 1.7 copy-done.11
  242.3 9.6 %convolution_bitcast_fusion.2 = f32[2,768,2048]{1,2,0:T(8,128)S(1)} fusion(bf16[2,768,1024]{2,1,0:T(8,128)(2,1)} %get-tuple-element.152, bf16[12288,1024]{1,0:T(8,128)(2,1)} %get-tuple-element.151, s32[]{:T(128)S(6)} %select_n.160), kind=kOutput, calls=%fused_computation.2.clone.1 | convolution fusion | flops 6442450944 | bytes 19922948 | tf_op jit(solution)/shard_map/while/body/eval_jaxpr/qoa,ba->qob/dot_general | solution.py:57
  251.9 5.7 %select_add_fusion.2 = f32[768,1024]{1,0:T(8,128)S(1)} fusion(f32[768,1024]{1,0:T(8,128)S(1)} %copy-done.10, bf16[12288,1024]{1,0:T(8,128)(2,1)} %get-tuple-element.151, s32[]{:T(128)S(6)} %select_n.160, f32[2,768,2048]{1,2,0:T(8,128)S(1)} %convolution_bitcast_fusion.2, pred[]{:T(512)S(6)} %compare.19), kind=kOutput, calls=%fused_computation.8.clone.1 | convolution fusion | flops 3225944064 | bytes 23068676 | tf_op jit(solution)/shard_map/while/body/eval_jaxpr/dot_general | solution.py:61
  257.6 1.7 copy-done.11
  259.3 9.6 %convolution_bitcast_fusion.2 = f32[2,768,2048]{1,2,0:T(8,128)S(1)} fusion(bf16[2,768,1024]{2,1,0:T(8,128)(2,1)} %get-tuple-element.152, bf16[12288,1024]{1,0:T(8,128)(2,1)} %get-tuple-element.151, s32[]{:T(128)S(6)} %select_n.160), kind=kOutput, calls=%fused_computation.2.clone.1 | convolution fusion | flops 6442450944 | bytes 19922948 | tf_op jit(solution)/shard_map/while/body/eval_jaxpr/qoa,ba->qob/dot_general | solution.py:57
  268.9 5.7 %select_add_fusion.2 = f32[768,1024]{1,0:T(8,128)S(1)} fusion(f32[768,1024]{1,0:T(8,128)S(1)} %copy-done.10, bf16[12288,1024]{1,0:T(8,128)(2,1)} %get-tuple-element.151, s32[]{:T(128)S(6)} %select_n.160, f32[2,768,2048]{1,2,0:T(8,128)S(1)} %convolution_bitcast_fusion.2, pred[]{:T(512)S(6)} %compare.19), kind=kOutput, calls=%fused_computation.8.clone.1 | convolution fusion | flops 3225944064 | bytes 23068676 | tf_op jit(solution)/shard_map/while/body/eval_jaxpr/dot_general | solution.py:61
  274.5 1.7 copy-done.11
  276.2 9.6 %convolution_bitcast_fusion.2 = f32[2,768,2048]{1,2,0:T(8,128)S(1)} fusion(bf16[2,768,1024]{2,1,0:T(8,128)(2,1)} %get-tuple-element.152, bf16[12288,1024]{1,0:T(8,128)(2,1)} %get-tuple-element.151, s32[]{:T(128)S(6)} %select_n.160), kind=kOutput, calls=%fused_computation.2.clone.1 | convolution fusion | flops 6442450944 | bytes 19922948 | tf_op jit(solution)/shard_map/while/body/eval_jaxpr/qoa,ba->qob/dot_general | solution.py:57
  285.8 5.7 %select_add_fusion.2 = f32[768,1024]{1,0:T(8,128)S(1)} fusion(f32[768,1024]{1,0:T(8,128)S(1)} %copy-done.10, bf16[12288,1024]{1,0:T(8,128)(2,1)} %get-tuple-element.151, s32[]{:T(128)S(6)} %select_n.160, f32[2,768,2048]{1,2,0:T(8,128)S(1)} %convolution_bitcast_fusion.2, pred[]{:T(512)S(6)} %compare.19), kind=kOutput, calls=%fused_computation.8.clone.1 | convolution fusion | flops 3225944064 | bytes 23068676 | tf_op jit(solution)/shard_map/while/body/eval_jaxpr/dot_general | solution.py:61
  291.5 1.7 copy-done.11
  293.2 9.6 %convolution_bitcast_fusion.2 = f32[2,768,2048]{1,2,0:T(8,128)S(1)} fusion(bf16[2,768,1024]{2,1,0:T(8,128)(2,1)} %get-tuple-element.152, bf16[12288,1024]{1,0:T(8,128)(2,1)} %get-tuple-element.151, s32[]{:T(128)S(6)} %select_n.160), kind=kOutput, calls=%fused_computation.2.clone.1 | convolution fusion | flops 6442450944 | bytes 19922948 | tf_op jit(solution)/shard_map/while/body/eval_jaxpr/qoa,ba->qob/dot_general | solution.py:57
  302.8 5.7 %select_add_fusion.2 = f32[768,1024]{1,0:T(8,128)S(1)} fusion(f32[768,1024]{1,0:T(8,128)S(1)} %copy-done.10, bf16[12288,1024]{1,0:T(8,128)(2,1)} %get-tuple-element.151, s32[]{:T(128)S(6)} %select_n.160, f32[2,768,2048]{1,2,0:T(8,128)S(1)} %convolution_bitcast_fusion.2, pred[]{:T(512)S(6)} %compare.19), kind=kOutput, calls=%fused_computation.8.clone.1 | convolution fusion | flops 3225944064 | bytes 23068676 | tf_op jit(solution)/shard_map/while/body/eval_jaxpr/dot_general | solution.py:61
  308.5 1.7 copy-done.11
  310.2 9.6 %convolution_bitcast_fusion.2 = f32[2,768,2048]{1,2,0:T(8,128)S(1)} fusion(bf16[2,768,1024]{2,1,0:T(8,128)(2,1)} %get-tuple-element.152, bf16[12288,1024]{1,0:T(8,128)(2,1)} %get-tuple-element.151, s32[]{:T(128)S(6)} %select_n.160), kind=kOutput, calls=%fused_computation.2.clone.1 | convolution fusion | flops 6442450944 | bytes 19922948 | tf_op jit(solution)/shard_map/while/body/eval_jaxpr/qoa,ba->qob/dot_general | solution.py:57
  319.8 5.7 %select_add_fusion.2 = f32[768,1024]{1,0:T(8,128)S(1)} fusion(f32[768,1024]{1,0:T(8,128)S(1)} %copy-done.10, bf16[12288,1024]{1,0:T(8,128)(2,1)} %get-tuple-element.151, s32[]{:T(128)S(6)} %select_n.160, f32[2,768,2048]{1,2,0:T(8,128)S(1)} %convolution_bitcast_fusion.2, pred[]{:T(512)S(6)} %compare.19), kind=kOutput, calls=%fused_computation.8.clone.1 | convolution fusion | flops 3225944064 | bytes 23068676 | tf_op jit(solution)/shard_map/while/body/eval_jaxpr/dot_general | solution.py:61
  325.5 1.7 copy-done.11
  327.1 5.7 %fusion.45 = f32[1024,1024]{1,0:T(8,128)} fusion(bf16[768,1024]{1,0:T(8,128)(2,1)S(1)} %copy-done.1, f32[768,1024]{1,0:T(8,128)} %get-tuple-element.84), kind=kOutput, calls=%fused_computation.44 | convolution fusion | flops 1611399168 | bytes 8912896 | tf_op jit(solution)/shard_map/tsk,sl->ktl/dot_general | solution.py:82
  333.1 75.7 %reduce-scatter.3.cloned.1.call-done = f32[64,1024]{1,0:T(8,128)} async-done(((f32[1024,1024]{1,0:T(8,128)}), f32[64,1024]{1,0:T(8,128)}) %reduce-scatter.3.cloned.1.call-update) | async-done | bytes 262160 | tf_op jit(solution)/shard_map/reduce_scatter | solution.py:81
  408.8 1.9 multiply_multiply_fusion
  410.8 14.1 %reduce-scatter.5.cloned.1.call-done = f32[1,64,1024]{2,1,0:T(8,128)} async-done(((f32[2,64,1024]{2,1,0:T(8,128)}), f32[1,64,1024]{2,1,0:T(8,128)}) %reduce-scatter.5.cloned.1.call-update) | async-done | bytes 262160 | tf_op jit(solution)/shard_map/reduce_scatter | solution.py:90
  (102 shorter events, 24.5 us)
Async XLA Ops:
  6.5 326.4 %copy-start = (f32[2,2]{1,0:T(2,128)S(1)}, f32[2,2]{1,0:T(2,128)}, u32[]{:S(2)}) copy-start(f32[2,2]{1,0:T(2,128)} %param.9) | copy-start | bytes 52
  6.5 96.5 %copy-start.1 = (bf16[768,1024]{1,0:T(8,128)(2,1)S(1)}, bf16[768,1024]{1,0:T(8,128)(2,1)}, u32[]{:S(2)}) copy-start(bf16[768,1024]{1,0:T(8,128)(2,1)} %param.8) | copy-start | bytes 4718596
  6.5 96.5 %copy-start.2 = (bf16[1,64,1024]{2,1,0:T(8,128)(2,1)S(1)}, bf16[1,64,1024]{2,1,0:T(8,128)(2,1)}, u32[]{:S(2)}) copy-start(bf16[1,64,1024]{2,1,0:T(8,128)(2,1)} %param.7) | copy-start | bytes 393220
  6.5 96.5 %copy-start.3 = (bf16[1,64,1024]{2,1,0:T(8,128)(2,1)S(1)}, bf16[1,64,1024]{2,1,0:T(8,128)(2,1)}, u32[]{:S(2)}) copy-start(bf16[1,64,1024]{2,1,0:T(8,128)(2,1)} %param.6) | copy-start | bytes 393220
  6.5 218.8 %all-gather.2.cloned.1.call-start = ((), (), s32[]{:S(2)}) async-start(), calls=%async_computation.2 | async-start | bytes 26738688 | tf_op jit(solution)/shard_map/all_gather | solution.py:79
  7.3 401.6 %reduce-scatter.3.cloned.1.call-start = ((), (), s32[]{:S(2)}) async-start(), calls=%async_computation.3 | async-start | bytes 4456448 | tf_op jit(solution)/shard_map/reduce_scatter | solution.py:81
  8.3 9.6 %collective-permute-start = (bf16[2,1,64,1024]{3,2,0,1:T(8,128)(2,1)S(1)}, bf16[2,1,64,1024]{3,2,0,1:T(8,128)(2,1)S(1)}, u32[]{:S(2)}, u32[]{:S(2)}) collective-permute-start(bf16[2,1,64,1024]{3,2,0,1:T(8,128)(2,1)S(1)} %pad_maximum_fusion), channel_id=1, source_target_pairs={{0,1},{1,2},{2,3},{3,4},{4,5},{5,6},{6,7},{7,8},{8,9},{9,10},{10,1... | collective-permute-start | bytes 786440 | tf_op jit(solution)/shard_map/ppermute | solution.py:16
  17.9 0.7 copy-start.7
  17.9 13.9 %collective-permute-start.1 = (bf16[2,1,64,1024]{3,2,0,1:T(8,128)(2,1)S(1)}, bf16[2,1,64,1024]{3,2,0,1:T(8,128)(2,1)S(1)}, u32[]{:S(2)}, u32[]{:S(2)}) collective-permute-start(bf16[2,1,64,1024]{3,2,0,1:T(8,128)(2,1)S(1)} %collective-permute-done), channel_id=1, source_target_pairs={{0,1},{1,2},{2,3},{3,4},{4,5},{5,6},{6,7},{7,8},{8,9},{9,10},{10,1... | collective-permute-start | bytes 786440 | tf_op jit(solution)/shard_map/ppermute | solution.py:16
  31.8 0.7 copy-start.9
  31.8 14.2 %collective-permute-start.2 = (bf16[2,1,64,1024]{3,2,0,1:T(8,128)(2,1)S(1)}, bf16[2,1,64,1024]{3,2,0,1:T(8,128)(2,1)S(1)}, u32[]{:S(2)}, u32[]{:S(2)}) collective-permute-start(bf16[2,1,64,1024]{3,2,0,1:T(8,128)(2,1)S(1)} %collective-permute-done.1), channel_id=1, source_target_pairs={{0,1},{1,2},{2,3},{3,4},{4,5},{5,6},{6,7},{7,8},{8,9},{9,10},{10,1... | collective-permute-start | bytes 786440 | tf_op jit(solution)/shard_map/ppermute | solution.py:16
  46.0 28.5 %copy-start.6 = (bf16[2,1,64,1024]{3,2,0,1:T(8,128)(2,1)}, bf16[2,1,64,1024]{3,2,0,1:T(8,128)(2,1)S(1)}, u32[]{:S(2)}) copy-start(bf16[2,1,64,1024]{3,2,0,1:T(8,128)(2,1)S(1)} %collective-permute-done.2) | copy-start | bytes 786436
  46.0 14.2 %collective-permute-start.3 = (bf16[2,1,64,1024]{3,2,0,1:T(8,128)(2,1)S(1)}, bf16[2,1,64,1024]{3,2,0,1:T(8,128)(2,1)S(1)}, u32[]{:S(2)}, u32[]{:S(2)}) collective-permute-start(bf16[2,1,64,1024]{3,2,0,1:T(8,128)(2,1)S(1)} %collective-permute-done.2), channel_id=1, source_target_pairs={{0,1},{1,2},{2,3},{3,4},{4,5},{5,6},{6,7},{7,8},{8,9},{9,10},{10,1... | collective-permute-start | bytes 786440 | tf_op jit(solution)/shard_map/ppermute | solution.py:16
  60.3 28.5 %copy-start.4 = (bf16[2,1,64,1024]{3,2,0,1:T(8,128)(2,1)}, bf16[2,1,64,1024]{3,2,0,1:T(8,128)(2,1)S(1)}, u32[]{:S(2)}) copy-start(bf16[2,1,64,1024]{3,2,0,1:T(8,128)(2,1)S(1)} %collective-permute-done.3) | copy-start | bytes 786436
  60.3 14.2 %collective-permute-start.4 = (bf16[2,1,64,1024]{3,2,0,1:T(8,128)(2,1)S(1)}, bf16[2,1,64,1024]{3,2,0,1:T(8,128)(2,1)S(1)}, u32[]{:S(2)}, u32[]{:S(2)}) collective-permute-start(bf16[2,1,64,1024]{3,2,0,1:T(8,128)(2,1)S(1)} %collective-permute-done.3), channel_id=1, source_target_pairs={{0,1},{1,2},{2,3},{3,4},{4,5},{5,6},{6,7},{7,8},{8,9},{9,10},{10,1... | collective-permute-start | bytes 786440 | tf_op jit(solution)/shard_map/ppermute | solution.py:16
  74.5 14.2 %collective-permute-start.5 = (bf16[2,1,64,1024]{3,2,0,1:T(8,128)(2,1)S(1)}, bf16[2,1,64,1024]{3,2,0,1:T(8,128)(2,1)S(1)}, u32[]{:S(2)}, u32[]{:S(2)}) collective-permute-start(bf16[2,1,64,1024]{3,2,0,1:T(8,128)(2,1)S(1)} %collective-permute-done.4), channel_id=1, source_target_pairs={{0,1},{1,2},{2,3},{3,4},{4,5},{5,6},{6,7},{7,8},{8,9},{9,10},{10,1... | collective-permute-start | bytes 786440 | tf_op jit(solution)/shard_map/ppermute | solution.py:16
  88.7 14.2 %collective-permute-start.6 = (bf16[2,1,64,1024]{3,2,0,1:T(8,128)(2,1)S(1)}, bf16[2,1,64,1024]{3,2,0,1:T(8,128)(2,1)S(1)}, u32[]{:S(2)}, u32[]{:S(2)}) collective-permute-start(bf16[2,1,64,1024]{3,2,0,1:T(8,128)(2,1)S(1)} %collective-permute-done.5), channel_id=1, source_target_pairs={{0,1},{1,2},{2,3},{3,4},{4,5},{5,6},{6,7},{7,8},{8,9},{9,10},{10,1... | collective-permute-start | bytes 786440 | tf_op jit(solution)/shard_map/ppermute | solution.py:16
  103.0 14.2 %collective-permute-start.7 = (bf16[2,1,64,1024]{3,2,0,1:T(8,128)(2,1)S(1)}, bf16[2,1,64,1024]{3,2,0,1:T(8,128)(2,1)S(1)}, u32[]{:S(2)}, u32[]{:S(2)}) collective-permute-start(bf16[2,1,64,1024]{3,2,0,1:T(8,128)(2,1)S(1)} %collective-permute-done.6), channel_id=1, source_target_pairs={{0,1},{1,2},{2,3},{3,4},{4,5},{5,6},{6,7},{7,8},{8,9},{9,10},{10,1... | collective-permute-start | bytes 786440 | tf_op jit(solution)/shard_map/ppermute | solution.py:16
  104.0 13.2 %copy-start.8 = (bf16[2,1,64,1024]{3,2,0,1:T(8,128)(2,1)S(1)}, bf16[2,1,64,1024]{3,2,0,1:T(8,128)(2,1)}, u32[]{:S(2)}) copy-start(bf16[2,1,64,1024]{3,2,0,1:T(8,128)(2,1)} %copy-done.7) | copy-start | bytes 786436
  117.2 14.3 %collective-permute-start.8 = (bf16[2,1,64,1024]{3,2,0,1:T(8,128)(2,1)S(1)}, bf16[2,1,64,1024]{3,2,0,1:T(8,128)(2,1)}, u32[]{:S(2)}, u32[]{:S(2)}) collective-permute-start(bf16[2,1,64,1024]{3,2,0,1:T(8,128)(2,1)S(1)} %collective-permute-done.7), channel_id=1, source_target_pairs={{0,1},{1,2},{2,3},{3,4},{4,5},{5,6},{6,7},{7,8},{8,9},{9,10},{10,1... | collective-permute-start | bytes 786440 | tf_op jit(solution)/shard_map/ppermute | solution.py:16
  130.7 9.1 %copy-start.5 = (bf16[2,1,64,1024]{3,2,0,1:T(8,128)(2,1)S(1)}, bf16[2,1,64,1024]{3,2,0,1:T(8,128)(2,1)}, u32[]{:S(2)}) copy-start(bf16[2,1,64,1024]{3,2,0,1:T(8,128)(2,1)} %copy-done.4) | copy-start | bytes 786436
  131.6 14.7 %collective-permute-start.9 = (bf16[2,1,64,1024]{3,2,0,1:T(8,128)(2,1)}, bf16[2,1,64,1024]{3,2,0,1:T(8,128)(2,1)}, u32[]{:S(2)}, u32[]{:S(2)}) collective-permute-start(bf16[2,1,64,1024]{3,2,0,1:T(8,128)(2,1)} %collective-permute-done.8), channel_id=1, source_target_pairs={{0,1},{1,2},{2,3},{3,4},{4,5},{5,6},{6,7},{7,8},{8,9},{9,10},{10,1... | collective-permute-start | bytes 786440 | tf_op jit(solution)/shard_map/ppermute | solution.py:16
  146.2 14.5 %collective-permute-start.10 = (bf16[2,1,64,1024]{3,2,0,1:T(8,128)(2,1)}, bf16[2,1,64,1024]{3,2,0,1:T(8,128)(2,1)S(1)}, u32[]{:S(2)}, u32[]{:S(2)}) collective-permute-start(bf16[2,1,64,1024]{3,2,0,1:T(8,128)(2,1)} %collective-permute-done.9), channel_id=1, source_target_pairs={{0,1},{1,2},{2,3},{3,4},{4,5},{5,6},{6,7},{7,8},{8,9},{9,10},{10,1... | collective-permute-start | bytes 786440 | tf_op jit(solution)/shard_map/ppermute | solution.py:16
  160.7 13.6 %collective-permute-start.11 = (bf16[2,1,64,1024]{3,2,0,1:T(8,128)(2,1)S(1)}, bf16[2,1,64,1024]{3,2,0,1:T(8,128)(2,1)S(1)}, u32[]{:S(2)}, u32[]{:S(2)}) collective-permute-start(bf16[2,1,64,1024]{3,2,0,1:T(8,128)(2,1)S(1)} %collective-permute-done.10), channel_id=1, source_target_pairs={{0,1},{1,2},{2,3},{3,4},{4,5},{5,6},{6,7},{7,8},{8,9},{9,10},{10,1... | collective-permute-start | bytes 786440 | tf_op jit(solution)/shard_map/ppermute | solution.py:16
  174.3 15.5 %collective-permute-start.12 = (bf16[2,1,64,1024]{3,2,0,1:T(8,128)(2,1)S(1)}, bf16[2,1,64,1024]{3,2,0,1:T(8,128)(2,1)S(1)}, u32[]{:S(2)}, u32[]{:S(2)}) collective-permute-start(bf16[2,1,64,1024]{3,2,0,1:T(8,128)(2,1)S(1)} %collective-permute-done.11), channel_id=1, source_target_pairs={{0,1},{1,2},{2,3},{3,4},{4,5},{5,6},{6,7},{7,8},{8,9},{9,10},{10,1... | collective-permute-start | bytes 786440 | tf_op jit(solution)/shard_map/ppermute | solution.py:16
  189.8 13.6 %collective-permute-start.13 = (bf16[2,1,64,1024]{3,2,0,1:T(8,128)(2,1)S(1)}, bf16[2,1,64,1024]{3,2,0,1:T(8,128)(2,1)}, u32[]{:S(2)}, u32[]{:S(2)}) collective-permute-start(bf16[2,1,64,1024]{3,2,0,1:T(8,128)(2,1)S(1)} %collective-permute-done.12), channel_id=1, source_target_pairs={{0,1},{1,2},{2,3},{3,4},{4,5},{5,6},{6,7},{7,8},{8,9},{9,10},{10,1... | collective-permute-start | bytes 786440 | tf_op jit(solution)/shard_map/ppermute | solution.py:16
  203.5 14.6 %collective-permute-start.14 = (bf16[2,1,64,1024]{3,2,0,1:T(8,128)(2,1)}, bf16[2,1,64,1024]{3,2,0,1:T(8,128)(2,1)S(1)}, u32[]{:S(2)}, u32[]{:S(2)}) collective-permute-start(bf16[2,1,64,1024]{3,2,0,1:T(8,128)(2,1)} %collective-permute-done.13), channel_id=1, source_target_pairs={{0,1},{1,2},{2,3},{3,4},{4,5},{5,6},{6,7},{7,8},{8,9},{9,10},{10,1... | collective-permute-start | bytes 786440 | tf_op jit(solution)/shard_map/ppermute | solution.py:16
  225.3 9.6 %copy-start.10 = (f32[768,1024]{1,0:T(8,128)S(1)}, f32[768,1024]{1,0:T(8,128)}, u32[]{:S(2)}) copy-start(f32[768,1024]{1,0:T(8,128)} %get-tuple-element.142) | copy-start | bytes 9437188 | tf_op jit(solution)/shard_map/while
  240.6 1.7 copy-start.11
  242.3 9.6 %copy-start.10 = (f32[768,1024]{1,0:T(8,128)S(1)}, f32[768,1024]{1,0:T(8,128)}, u32[]{:S(2)}) copy-start(f32[768,1024]{1,0:T(8,128)} %get-tuple-element.142) | copy-start | bytes 9437188 | tf_op jit(solution)/shard_map/while
  257.6 1.7 copy-start.11
  259.3 9.6 %copy-start.10 = (f32[768,1024]{1,0:T(8,128)S(1)}, f32[768,1024]{1,0:T(8,128)}, u32[]{:S(2)}) copy-start(f32[768,1024]{1,0:T(8,128)} %get-tuple-element.142) | copy-start | bytes 9437188 | tf_op jit(solution)/shard_map/while
  274.5 1.7 copy-start.11
  276.2 9.6 %copy-start.10 = (f32[768,1024]{1,0:T(8,128)S(1)}, f32[768,1024]{1,0:T(8,128)}, u32[]{:S(2)}) copy-start(f32[768,1024]{1,0:T(8,128)} %get-tuple-element.142) | copy-start | bytes 9437188 | tf_op jit(solution)/shard_map/while
  291.5 1.7 copy-start.11
  293.2 9.6 %copy-start.10 = (f32[768,1024]{1,0:T(8,128)S(1)}, f32[768,1024]{1,0:T(8,128)}, u32[]{:S(2)}) copy-start(f32[768,1024]{1,0:T(8,128)} %get-tuple-element.142) | copy-start | bytes 9437188 | tf_op jit(solution)/shard_map/while
  308.5 1.7 copy-start.11
  310.2 9.6 %copy-start.10 = (f32[768,1024]{1,0:T(8,128)S(1)}, f32[768,1024]{1,0:T(8,128)}, u32[]{:S(2)}) copy-start(f32[768,1024]{1,0:T(8,128)} %get-tuple-element.142) | copy-start | bytes 9437188 | tf_op jit(solution)/shard_map/while
  325.4 1.7 copy-start.11
  332.9 91.9 %reduce-scatter.5.cloned.1.call-start = ((), (), s32[]{:S(2)}) async-start(), calls=%async_computation.4 | async-start | bytes 786432 | tf_op jit(solution)/shard_map/reduce_scatter | solution.py:90
Sparse Core Ops, SparseCore 0:
  8.9 159.3 all-gather.1
  333.0 75.7 reduce-scatter.2
  411.1 13.6 reduce-scatter.4
